TPU v7x, 128 devices: a whole 4x4x4 slice. The times are simulated.
128 devices in a mesh: vae: 8 (over x_hi, z), seq: 16 (over x_lo, y, core).
Axes of the slice: x: 4 (x_hi: 2, x_lo: 2; x = x_hi * 2 + x_lo), y: 4, z: 4, core: 2. Of those that a mesh axis runs over, the one named last changes fastest.
Arguments:
- video: float32 [32, 256, 512], P('vae', 'seq')
- frame_counts: int32 [8], replicated, may hold values from 2 to 4, as said below
- conv_weight: float32 [3, 512, 512], replicated, may hold values from -0.15625 to 0.15625
- conv_bias: float32 [512], replicated, may hold values from -4 to 4
- norm_gain: float32 [512], replicated, may hold values from 0.1 to 1.9
- norm_bias: float32 [512], replicated, may hold values from -3 to 3
- embed_weight: bfloat16 [512, 3072], replicated, may hold values from -0.25 to 0.25
- embed_bias: float32 [3072], replicated, may hold values from -3 to 3
- shift: float32 [3072], replicated, may hold values from -3 to 3
- scale: float32 [3072], replicated, may hold values from -3 to 3
- gate: float32 [3072], replicated, may hold values from 1 to 3
- qkv_weight: bfloat16 [3072, 3, 3072], P(None, None, 'vae')
- q_gain: float32 [128], replicated, may hold values from 1 to 6
- k_gain: float32 [128], replicated, may hold values from 1 to 6
- out_weight: bfloat16 [3072, 3072], P('vae'), may hold values from -0.109375 to 0.109375
Outputs:
- result: bfloat16 [32, 256, 3072], P(None, 'seq', 'vae')
Inputs may be any that keep to these rules, and one draw needn't show every extreme that they name: `frame_counts`: every index of vae has at least 2 live slots; at least one has all 4 live.
All inputs are finite; a program needn't handle non-finite values.
Results may differ from a plain program's by a relative error of at most 0.013.
The roundings to bfloat16 on the way count: a program that leaves them out, or rounds other values in their place, can miss the bound.
Values may be sent and summed in bfloat16 or wider, within the bound.
A program may use at most 192 MiB of HBM per device.

v0:
```python
import math
import jax
import jax.numpy as jnp
from jax import lax
from jax.sharding import PartitionSpec as P

GROUPS = 32
HD = 128


def from_behind(x, axis, by):
    count = lax.axis_size(axis)
    pairs = [(i, i + by) for i in range(count) if 0 <= i + by < count]
    return lax.ppermute(x, axis, pairs)


def head_norm(values, weights):
    return values * lax.rsqrt(jnp.mean(values * values, axis=-1, keepdims=True) + 1e-06) * weights


def body(
    video,
    frame_counts,
    conv_weight,
    conv_bias,
    norm_gain,
    norm_bias,
    embed_weight,
    embed_bias,
    shift,
    scale,
    gate,
    qkv_weight,
    q_gain,
    k_gain,
    out_weight,
):
    highest = lax.Precision.HIGHEST
    fdev, pdev, chans = video.shape
    nvae = lax.axis_size("vae")
    nseq = lax.axis_size("seq")
    me_vae = lax.axis_index("vae")
    mine = frame_counts[me_vae]
    tail = lax.dynamic_slice_in_dim(video, mine - 2, 2, 0)
    prior = from_behind(tail, "vae", 1)
    extended = jnp.concatenate([prior, video], 0)
    conv = conv_bias + jnp.zeros((fdev, pdev, chans), jnp.float32)
    for tap in range(3):
        conv = conv + jnp.einsum(
            "fpc,cd->fpd", extended[2 - tap : 2 - tap + fdev], conv_weight[tap], precision=highest
        )
    local_live = (jnp.arange(fdev) < mine).astype(jnp.float32)[:, None, None]
    masked = conv * local_live
    width = chans // GROUPS
    first = masked.reshape(fdev, pdev, GROUPS, width).sum((0, 1, 3))
    second = (masked * conv).reshape(fdev, pdev, GROUPS, width).sum((0, 1, 3))
    first, second = lax.psum((first, second), ("vae", "seq"))
    number = jnp.sum(frame_counts).astype(jnp.float32) * (pdev * nseq * width)
    mean = first / number
    var = second / number - mean * mean
    centre = jnp.repeat(mean, width)
    inverse = jnp.repeat(lax.rsqrt(var + 1e-06), width)
    act = jax.nn.silu((conv - centre) * inverse * norm_gain + norm_bias).astype(jnp.bfloat16)
    frames_total = fdev * nvae
    slot_live = (jnp.arange(frames_total) % fdev < jnp.repeat(frame_counts, fdev)).astype(
        jnp.float32
    )
    count_frames = act.shape[0]
    projected = (
        jnp.dot(act.reshape(-1, chans), embed_weight, preferred_element_type=jnp.float32)
        + embed_bias
    )
    alive = lax.dynamic_slice_in_dim(slot_live, me_vae * fdev, count_frames, 0)
    own_tokens = (projected.reshape(count_frames, pdev, -1) * alive[:, None, None]).astype(
        jnp.bfloat16
    )
    tokens = lax.all_gather(own_tokens, "vae", axis=0, tiled=True)
    nloc = frames_total * pdev
    dwidth = tokens.shape[2]
    rows = tokens.reshape(nloc, dwidth).astype(jnp.float32)
    centred = rows - jnp.mean(rows, axis=-1, keepdims=True)
    spread = jnp.mean(centred * centred, axis=-1, keepdims=True)
    hidden = (centred * lax.rsqrt(spread + 1e-06) * (1.0 + scale) + shift).astype(jnp.bfloat16)
    proj = jnp.dot(hidden, qkv_weight.reshape(dwidth, -1), preferred_element_type=jnp.float32)
    inner = qkv_weight.shape[2]
    heads = inner // HD
    queries = head_norm(proj[:, :inner].reshape(nloc, heads, HD), q_gain).astype(jnp.bfloat16)
    keys = head_norm(proj[:, inner : 2 * inner].reshape(nloc, heads, HD), k_gain).astype(
        jnp.bfloat16
    )
    values = proj[:, 2 * inner :].reshape(nloc, heads, HD).astype(jnp.bfloat16)
    key_live = jnp.repeat(slot_live, pdev)
    root = math.sqrt(HD)
    best = jnp.full((heads, nloc), -1e30, jnp.float32)
    key_piece = lax.all_gather(keys, "seq", axis=0, tiled=True)
    value_piece = lax.all_gather(values, "seq", axis=0, tiled=True)
    length = key_piece.shape[0]
    alive = jnp.take(key_live, jnp.arange(length) % nloc) > 0.5
    scores = (
        jnp.einsum("nhd,khd->hnk", queries, key_piece, preferred_element_type=jnp.float32) / root
    )
    scores = jnp.where(alive[None, None, :], scores, -1e30)
    top = jnp.maximum(best, jnp.max(scores, axis=-1))
    weights = jnp.where(alive[None, None, :], jnp.exp(scores - top[..., None]), 0.0)
    summed = jnp.sum(weights, axis=-1)
    accum = jnp.einsum(
        "hnk,khd->nhd",
        weights.astype(jnp.bfloat16),
        value_piece,
        preferred_element_type=jnp.float32,
    )
    best, summed, accum = (top, summed, accum)
    attended = accum / jnp.transpose(summed, (1, 0))[..., None]
    merged = attended.reshape(nloc, inner).astype(jnp.bfloat16)
    partial_out = jnp.dot(merged, out_weight, preferred_element_type=jnp.float32)
    mixed = lax.psum_scatter(partial_out, "vae", scatter_dimension=1, tiled=True)
    columns = mixed.shape[1]
    residual = lax.dynamic_slice_in_dim(rows, me_vae * columns, columns, 1)
    gate_part = lax.dynamic_slice_in_dim(gate, me_vae * columns, columns, 0)
    result = ((residual + gate_part * mixed) * key_live[:, None]).astype(jnp.bfloat16)
    return result.reshape(frames_total, pdev, columns)


def solution(mesh):
    in_specs = (
        P("vae", "seq", None),
        P(),
        P(),
        P(),
        P(),
        P(),
        P(),
        P(),
        P(),
        P(),
        P(),
        P(None, None, "vae"),
        P(),
        P(),
        P("vae", None),
    )
    out_specs = P(None, "seq", "vae")
    return jax.shard_map(body, mesh=mesh, in_specs=in_specs, out_specs=out_specs, check_vma=False)
```

profile of v0, /device:TPU:0, one launch (start us, length us, event | category | flops | bytes accessed | tf_op | source)
XLA Modules:
  0.0 400.2 jit_solution(12064693817004700212)
XLA Ops:
  6.5 1.4 dynamic_slice.15
  9.2 0.8 constant_dynamic-slice_fusion
  10.1 3.9 collective-permute-start
  14.0 1.4 reduce_sum.89
  16.1 0.7 broadcast_in_dim.60
  16.9 2.0 convolution_add_fusion.1
  19.6 0.9 constant_dynamic-update-slice_fusion
  20.5 2.0 fusion.10
  22.5 2.0 fusion.22
  24.9 65.9 %all-reduce = (f32[32]{0:T(128)S(1)}, f32[32]{0:T(128)S(1)}) all-reduce(f32[32]{0:T(128)S(1)} %reduce_sum.88, f32[32]{0:T(128)S(1)} %reduce_sum.92), channel_id=1, replica_groups=mesh['vae'=8,'seq'=16] {'vae','seq'}, use_global_device_ids=true, to_apply=%region_2.0 | all-reduce | flops 64 | bytes 512 | tf_op jit(solution)/shard_map/psum | solution.py:57
  91.1 0.8 multiply_convert_fusion.5
  91.9 1.4 convolution_add_fusion
  93.3 0.9 multiply_convert_fusion.3
  94.2 10.3 %copy.25 = bf16[3072,3,384]{0,2,1:T(8,128)(2,1)} copy(bf16[3072,3,384]{2,0,1:T(8,128)(2,1)} %param.26) | data formatting | bytes 14155776 | tf_op args[11]
  104.6 49.5 %all-gather.4.cloned.1.call-done = bf16[32,16,3072]{2,1,0:T(8,128)(2,1)} async-done(((bf16[4,16,3072]{2,1,0:T(8,128)(2,1)}), bf16[32,16,3072]{2,1,0:T(8,128)(2,1)}) %all-gather.4.cloned.1.call-update) | async-done | bytes 3145744 | tf_op jit(solution)/shard_map/all_gather | solution.py:77
  154.0 2.5 convert_reduce_fusion
  156.6 3.6 multiply_reduce_fusion
  160.2 1.7 add_convert_fusion
  161.9 4.3 %fusion.33 = f32[512,1152]{1,0:T(8,128)S(1)} fusion(bf16[512,3072]{1,0:T(8,128)(2,1)S(1)} %bitcast.49, bf16[3072,1152]{0,1:T(8,128)(2,1)S(1)} %bitcast.46), kind=kOutput, calls=%fused_computation.71 | convolution fusion | flops 3623878656 | bytes 12582912 | tf_op jit(solution)/shard_map/dot_general | solution.py:84
  166.3 1.3 copy-done.5
  168.3 1.0 multiply_convert_fusion.1
  169.4 1.2 slice.51
  170.5 0.9 copy.26
  172.0 51.2 %gather_fusion = f32[8192]{0:T(1024)S(1)} fusion(f32[512]{0:T(512)S(1)} %reshape.176, s32[8192]{0:T(1024)S(1)} %broadcast_clamp_fusion), kind=kCustom, calls=%fused_computation | custom fusion | bytes 98304 | tf_op jit(solution)/shard_map/jit(_take)/gather | solution.py:98
  223.6 21.7 %fusion = (f32[3,512]{1,0:T(4,128)S(1)}, f32[3,512,8192]{2,1,0:T(8,128)}) fusion(pred[8192]{0:T(1024)(128)(4,1)S(1)} %select_compare_fusion, bf16[8192,3,128]{2,0,1:T(8,128)(2,1)} %all-gather.8.cloned.1.call-done, f32[512,3,128]{0,2,1:T(8,128)S(1)} %bitcast.45, f32[128]{0:T(128)S(1)} %copy-done.6, f32[512,3]{0,1:T(4,128)S(1)} %add_rsqrt_fusion.2), kind=kOutput, calls=%fused_computation.3 | convolution fusion | flops 3259562496 | bytes 57430528 | tf_op jit(solution)/shard_map/nhd,khd->hnk/dot_general | solution.py:100
  245.3 23.2 %fusion.1 = f32[3,512]{1,0:T(4,128)S(1)} fusion(f32[3,512,8192]{2,1,0:T(8,128)} %get-tuple-element.15, f32[3,512]{1,0:T(4,128)S(1)} %broadcast_maximum_fusion, pred[8192]{0:T(1024)(128)(4,1)S(1)} %select_compare_fusion), kind=kLoop, calls=%fused_computation.4 | loop fusion | flops 62913024 | bytes 50352128 | tf_op jit(solution)/shard_map/reduce_sum | solution.py:105
  268.5 22.0 %divide_convert_fusion = bf16[512,3,128]{0,2,1:T(8,128)(2,1)S(1)} fusion(bf16[8192,3,128]{0,2,1:T(8,128)(2,1)} %all-gather.6.cloned.1.call-done, f32[3,512,8192]{2,1,0:T(8,128)} %get-tuple-element.15, f32[3,512]{1,0:T(4,128)S(1)} %broadcast_maximum_fusion, pred[8192]{0:T(1024)(128)(4,1)S(1)} %select_compare_fusion, f32[512,3]{0,1:T(4,128)S(1)} %bitcast.55), kind=kOutput, calls=%fused_computation.25 | convolution fusion | flops 3284533248 | bytes 57036800 | tf_op jit(solution)/shard_map/hnk,khd->nhd/dot_general | solution.py:106
  290.6 4.5 %fusion.34 = f32[512,3072]{1,0:T(8,128)} fusion(bf16[512,384]{0,1:T(8,128)(2,1)S(1)} %bitcast.52, bf16[384,3072]{1,0:T(8,128)(2,1)S(1)} %copy-done.4), kind=kOutput, calls=%fused_computation.72 | convolution fusion | flops 1207959552 | bytes 9043968 | tf_op jit(solution)/shard_map/dot_general | solution.py:115
  295.1 0.9 dynamic_slice.19
  296.0 5.4 %bitcast_convert_fusion = f32[512,3072]{1,0:T(8,128)} fusion(bf16[32,16,3072]{2,1,0:T(8,128)(2,1)} %all-gather.4.cloned.1.call-done), kind=kLoop, calls=%fused_computation.70 | loop fusion | flops 1572864 | bytes 9437184 | tf_op jit(solution)/shard_map/convert_element_type | solution.py:80
  301.4 90.0 %reduce-scatter.2.cloned.1.call-done = f32[512,384]{1,0:T(8,128)} async-done(((f32[512,3072]{1,0:T(8,128)}), f32[512,384]{1,0:T(8,128)}) %reduce-scatter.2.cloned.1.call-update) | async-done | bytes 786448 | tf_op jit(solution)/shard_map/reduce_scatter | solution.py:116
  391.4 2.3 multiply_convert_fusion
  (61 shorter events, 3.3 us)
Async XLA Ops:
  6.5 85.4 %copy-start = (bf16[512,3072]{1,0:T(8,128)(2,1)S(1)}, bf16[512,3072]{1,0:T(8,128)(2,1)}, u32[]{:S(2)}) copy-start(bf16[512,3072]{1,0:T(8,128)(2,1)} %param.21) | copy-start | bytes 9437188
  6.5 147.5 %all-gather.4.cloned.1.call-start = ((), (), s32[]{:S(2)}) async-start(), calls=%async_computation.1 | async-start | bytes 3538944 | tf_op jit(solution)/shard_map/all_gather | solution.py:77
  10.1 9.5 %collective-permute-start = (f32[2,16,512]{2,1,0:T(8,128)S(1)}, f32[2,16,512]{2,1,0:T(8,128)S(1)}, u32[]{:S(2)}, u32[]{:S(2)}) collective-permute-start(f32[2,16,512]{2,1,0:T(8,128)S(1)} %constant_dynamic-slice_fusion), channel_id=1, source_target_pairs={{0,16},{16,32},{32,48},{48,64},{64,80},{80,96},{96,112},{1,17},{17... | collective-permute-start | bytes 196616 | tf_op jit(solution)/shard_map/ppermute | solution.py:14
  94.2 10.4 %copy-start.8 = (f32[3072]{0:T(1024)S(1)}, f32[3072]{0:T(1024)}, u32[]{:S(2)}) copy-start(f32[3072]{0:T(1024)} %param.24) | copy-start | bytes 36868
  94.2 129.4 %all-gather.8.cloned.1.call-start = ((), (), s32[]{:S(2)}) async-start(), calls=%async_computation.3 | async-start | bytes 6684672 | tf_op jit(solution)/shard_map/all_gather | solution.py:95
  104.5 55.6 %copy-start.7 = (f32[3072]{0:T(1024)S(1)}, f32[3072]{0:T(1024)}, u32[]{:S(2)}) copy-start(f32[3072]{0:T(1024)} %param.23) | copy-start | bytes 36868
  154.0 6.2 %copy-start.2 = (bf16[32,16,3072]{2,1,0:T(8,128)(2,1)S(1)}, bf16[32,16,3072]{2,1,0:T(8,128)(2,1)}, u32[]{:S(2)}) copy-start(bf16[32,16,3072]{2,1,0:T(8,128)(2,1)} %all-gather.4.cloned.1.call-done) | copy-start | bytes 9437188
  154.0 7.9 %copy-start.3 = (bf16[3072,3,384]{0,2,1:T(8,128)(2,1)S(1)}, bf16[3072,3,384]{0,2,1:T(8,128)(2,1)}, u32[]{:S(2)}) copy-start(bf16[3072,3,384]{0,2,1:T(8,128)(2,1)} %copy.25) | copy-start | bytes 21233668
  166.2 1.4 copy-start.5
  166.2 2.1 copy-start.9
  169.3 99.2 %all-gather.6.cloned.1.call-start = ((), (), s32[]{:S(2)}) async-start(), calls=%async_computation.2 | async-start | bytes 6684672 | tf_op jit(solution)/shard_map/all_gather | solution.py:96
  171.5 219.9 %reduce-scatter.2.cloned.1.call-start = ((), (), s32[]{:S(2)}) async-start(), calls=%async_computation.4 | async-start | bytes 7077888 | tf_op jit(solution)/shard_map/reduce_scatter | solution.py:116
  171.9 51.7 %copy-start.6 = (f32[128]{0:T(128)S(1)}, f32[128]{0:T(128)}, u32[]{:S(2)}) copy-start(f32[128]{0:T(128)} %param.27) | copy-start | bytes 1540
  268.5 22.0 %copy-start.4 = (bf16[384,3072]{1,0:T(8,128)(2,1)S(1)}, bf16[384,3072]{1,0:T(8,128)(2,1)}, u32[]{:S(2)}) copy-start(bf16[384,3072]{1,0:T(8,128)(2,1)} %param.29) | copy-start | bytes 7077892
  295.1 98.6 %copy-start.1 = (bf16[512,3072]{1,0:T(8,128)(2,1)S(1)}, bf16[512,3072]{1,0:T(8,128)(2,1)}, u32[]{:S(2)}) copy-start(bf16[512,3072]{1,0:T(8,128)(2,1)} %param.21) | copy-start | bytes 9437188
Sparse Core Ops, SparseCore 0:
  94.3 59.7 all-gather.3
  169.4 40.0 all-gather.7
  211.2 43.1 all-gather.5
  295.2 96.1 reduce-scatter.1
where the time goes:
time: 401 us; the launch traced here: 400 us
  waiting for transfers between devices  140 us (35%)
  local copies, waits for them, and re-layouts  71.5 us (18%)
  blocking collectives  65.9 us (16%)
  matrix products  59.8 us (15%)
  other arithmetic  43.8 us (11%)
  between operations  15.4 us (4%)
  starting transfers between devices  4.23 us (1%)
    reduce_scatter x1, waiting for transfers between devices, body(): lax.psum_scatter(partial_out, 'vae', scatter_dimension=1, tiled=True)  90 us
    psum x1, blocking collectives, body(): first, second = lax.psum((first, second), ('vae', 'seq'))  65.9 us
    gather x1, local copies, waits for them, and re-layouts, body(): alive = jnp.take(key_live, jnp.arange(length) % nloc) > 0.5  51.2 us
    all_gather x1, waiting for transfers between devices, body(): tokens = lax.all_gather(own_tokens, 'vae', axis=0, tiled=True)  49.5 us
    reduce_sum x1, other arithmetic, body(): summed = jnp.sum(weights, axis=-1)  23.2 us
    dot_general x1, matrix products, body(): jnp.einsum('hnk,khd->nhd', weights.astype(jnp.bfloat16), value_piece, pre...  22 us
    dot_general x1, matrix products, body(): jnp.einsum('nhd,khd->hnk', queries, key_piece, preferred_element_type=jnp...  21.7 us
    unnamed x22, local copies, waits for them, and re-layouts  11.7 us
  transfers between devices with their start and end apart: 5, of which 2 were waited for; matrix products, arithmetic and copies ran while one was open for 30% of the time, Pallas kernels for 0%

commit v1 on v0

--- a/solution.py
+++ b/solution.py
@@ -74,7 +74,15 @@
     own_tokens = (projected.reshape(count_frames, pdev, -1) * alive[:, None, None]).astype(
         jnp.bfloat16
     )
-    tokens = lax.all_gather(own_tokens, "vae", axis=0, tiled=True)
+
+    def build_case(array_axis, packet):
+        arr_next = tuple((packet for _ in range(lax.axis_size("vae"))))
+        w1 = jnp.stack(arr_next)
+        out_arr = lax.all_to_all(w1, axis_name="vae", split_axis=0, concat_axis=0)
+        later = jnp.concatenate(out_arr, array_axis)
+        return later
+
+    tokens = build_case(0, own_tokens)
     nloc = frames_total * pdev
     dwidth = tokens.shape[2]
     rows = tokens.reshape(nloc, dwidth).astype(jnp.float32)

time: 401 us -> 381 us (0.950)
  waiting for transfers between devices: 140 us -> 117 us
  other arithmetic: 43.8 us -> 38.4 us
  starting transfers between devices: 4.23 us -> 8.89 us
    all_gather x1 -> x0, waiting for transfers between devices: 49.5 us -> none  [body(): tokens = lax.all_gather(own_tokens, 'vae', axis=0, tiled=True)]
    all_to_all x0 -> x1, waiting for transfers between devices: none -> 27.2 us  [build_case(): out_arr = lax.all_to_all(w1, axis_name='vae', split_axis=0, concat_axis=0)]
    all_to_all x0 -> x1, starting transfers between devices: none -> 4.45 us  [build_case(): out_arr = lax.all_to_all(w1, axis_name='vae', split_axis=0, concat_axis=0)]
  transfers between devices with their start and end apart: 5 -> 5, of which waited for: 2 -> 2; matrix products, arithmetic and copies ran while one was open for 30% -> 32% of each run, Pallas kernels for 0% -> 0%
where the time goes in v1:
time: 381 us; the launch traced here: 380 us
  waiting for transfers between devices  117 us (31%)
  local copies, waits for them, and re-layouts  74.4 us (20%)
  blocking collectives  65.9 us (17%)
  matrix products  59.8 us (16%)
  other arithmetic  38.4 us (10%)
  between operations  15.4 us (4%)
  starting transfers between devices  8.89 us (2%)
    reduce_scatter x1, waiting for transfers between devices, body(): lax.psum_scatter(partial_out, 'vae', scatter_dimension=1, tiled=True)  90.1 us
    psum x1, blocking collectives, body(): first, second = lax.psum((first, second), ('vae', 'seq'))  65.9 us
    gather x1, local copies, waits for them, and re-layouts, body(): alive = jnp.take(key_live, jnp.arange(length) % nloc) > 0.5  51.2 us
    all_to_all x1, waiting for transfers between devices, build_case(): out_arr = lax.all_to_all(w1, axis_name='vae', split_axis=0, concat_axis=0)  27.2 us
    reduce_sum x1, other arithmetic, body(): summed = jnp.sum(weights, axis=-1)  23.2 us
    dot_general x1, matrix products, body(): jnp.einsum('hnk,khd->nhd', weights.astype(jnp.bfloat16), value_piece, pre...  22 us
    dot_general x1, matrix products, body(): jnp.einsum('nhd,khd->hnk', queries, key_piece, preferred_element_type=jnp...  21.7 us
    unnamed x22, local copies, waits for them, and re-layouts  12.5 us
  transfers between devices with their start and end apart: 5, of which 2 were waited for; matrix products, arithmetic and copies ran while one was open for 32% of the time, Pallas kernels for 0%

profile of v1, /device:TPU:0, one launch (start us, length us, event | category | flops | bytes accessed | tf_op | source)
XLA Modules:
  0.0 380.2 jit_solution(11902690550081406978)
XLA Ops:
  6.5 1.4 dynamic_slice.15
  9.2 0.8 constant_dynamic-slice_fusion
  10.1 3.9 %collective-permute-start = (f32[2,16,512]{2,1,0:T(8,128)S(1)}, f32[2,16,512]{2,1,0:T(8,128)S(1)}, u32[]{:S(2)}, u32[]{:S(2)}) collective-permute-start(f32[2,16,512]{2,1,0:T(8,128)S(1)} %constant_dynamic-slice_fusion), channel_id=1, source_target_pairs={{0,16},{16,32},{32,48},{48,64},{64,80},{80,96},{96,112},{1,17},{17... | collective-permute-start | bytes 196616 | tf_op jit(solution)/shard_map/ppermute | solution.py:14
  14.0 1.4 reduce_sum.89
  16.9 2.0 convolution_add_fusion.1
  19.6 0.9 constant_dynamic-update-slice_fusion
  20.5 2.0 fusion.10
  22.5 2.0 fusion.22
  24.9 65.9 %all-reduce = (f32[32]{0:T(128)S(1)}, f32[32]{0:T(128)S(1)}) all-reduce(f32[32]{0:T(128)S(1)} %reduce_sum.88, f32[32]{0:T(128)S(1)} %reduce_sum.92), channel_id=1, replica_groups=mesh['vae'=8,'seq'=16] {'vae','seq'}, use_global_device_ids=true, to_apply=%region_2.0 | all-reduce | flops 64 | bytes 512 | tf_op jit(solution)/shard_map/psum | solution.py:57
  91.1 0.8 multiply_convert_fusion.5
  91.9 1.4 convolution_add_fusion
  93.4 2.1 stack.2
  95.5 4.4 %all-to-all-start = ((bf16[8,4,16,3072]{3,2,1,0:T(8,128)(2,1)}), bf16[8,4,16,3072]{3,2,1,0:T(8,128)(2,1)S(1)}, u32[]{:S(2)}, u32[]{:S(2)}) async-start(bf16[8,4,16,3072]{3,2,1,0:T(8,128)(2,1)} %stack.2), calls=%async_computation | async-start | bytes 6291456 | tf_op jit(solution)/shard_map/all_to_all | solution.py:81
  100.2 10.3 %copy.19 = bf16[3072,3,384]{0,2,1:T(8,128)(2,1)} copy(bf16[3072,3,384]{2,0,1:T(8,128)(2,1)} %param.26) | data formatting | bytes 14155776 | tf_op args[11]
  110.5 27.2 %all-to-all-done = bf16[8,4,16,3072]{3,2,1,0:T(8,128)(2,1)S(1)} async-done(((bf16[8,4,16,3072]{3,2,1,0:T(8,128)(2,1)}), bf16[8,4,16,3072]{3,2,1,0:T(8,128)(2,1)S(1)}, u32[]{:S(2)}, u32[]{:S(2)}) %all-to-all-start) | async-done | bytes 3145760 | tf_op jit(solution)/shard_map/all_to_all | solution.py:81
  138.1 1.0 multiply_reduce_fusion
  139.1 1.7 add_convert_fusion
  140.9 0.9 copy-done.3
  141.8 4.3 %fusion.33 = f32[512,1152]{1,0:T(8,128)S(1)} fusion(bf16[512,3072]{1,0:T(8,128)(2,1)S(1)} %bitcast.49, bf16[3072,1152]{0,1:T(8,128)(2,1)S(1)} %bitcast.46), kind=kOutput, calls=%fused_computation.71 | convolution fusion | flops 3623878656 | bytes 12582912 | tf_op jit(solution)/shard_map/dot_general | solution.py:92
  146.2 1.3 copy-done.5
  148.1 1.0 multiply_convert_fusion.1
  149.2 1.2 slice.51
  150.4 0.9 copy.20
  151.8 51.2 %gather_fusion = f32[8192]{0:T(1024)S(1)} fusion(f32[512]{0:T(512)S(1)} %reshape.178, s32[8192]{0:T(1024)S(1)} %broadcast_clamp_fusion), kind=kCustom, calls=%fused_computation | custom fusion | bytes 98304 | tf_op jit(solution)/shard_map/jit(_take)/gather | solution.py:106
  203.5 21.7 %fusion = (f32[3,512]{1,0:T(4,128)S(1)}, f32[3,512,8192]{2,1,0:T(8,128)}) fusion(pred[8192]{0:T(1024)(128)(4,1)S(1)} %select_compare_fusion, bf16[8192,3,128]{2,0,1:T(8,128)(2,1)} %all-gather.5.cloned.1.call-done, f32[512,3,128]{0,2,1:T(8,128)S(1)} %bitcast.45, f32[128]{0:T(128)S(1)} %copy-done.6, f32[512,3]{0,1:T(4,128)S(1)} %add_rsqrt_fusion.2), kind=kOutput, calls=%fused_computation.3 | convolution fusion | flops 3259562496 | bytes 57430528 | tf_op jit(solution)/shard_map/nhd,khd->hnk/dot_general | solution.py:108
  225.2 23.2 %fusion.1 = f32[3,512]{1,0:T(4,128)S(1)} fusion(f32[3,512,8192]{2,1,0:T(8,128)} %get-tuple-element.15, f32[3,512]{1,0:T(4,128)S(1)} %broadcast_maximum_fusion, pred[8192]{0:T(1024)(128)(4,1)S(1)} %select_compare_fusion), kind=kLoop, calls=%fused_computation.4 | loop fusion | flops 62913024 | bytes 50352128 | tf_op jit(solution)/shard_map/reduce_sum | solution.py:113
  248.4 22.0 %divide_convert_fusion = bf16[512,3,128]{0,2,1:T(8,128)(2,1)S(1)} fusion(bf16[8192,3,128]{0,2,1:T(8,128)(2,1)} %all-gather.3.cloned.1.call-done, f32[3,512,8192]{2,1,0:T(8,128)} %get-tuple-element.15, f32[3,512]{1,0:T(4,128)S(1)} %broadcast_maximum_fusion, pred[8192]{0:T(1024)(128)(4,1)S(1)} %select_compare_fusion, f32[512,3]{0,1:T(4,128)S(1)} %bitcast.55), kind=kOutput, calls=%fused_computation.25 | convolution fusion | flops 3284533248 | bytes 57036800 | tf_op jit(solution)/shard_map/hnk,khd->nhd/dot_general | solution.py:114
  270.4 4.5 %fusion.34 = f32[512,3072]{1,0:T(8,128)} fusion(bf16[512,384]{0,1:T(8,128)(2,1)S(1)} %bitcast.52, bf16[384,3072]{1,0:T(8,128)(2,1)S(1)} %copy-done.4), kind=kOutput, calls=%fused_computation.72 | convolution fusion | flops 1207959552 | bytes 9043968 | tf_op jit(solution)/shard_map/dot_general | solution.py:123
  275.0 0.9 dynamic_slice.19
  275.9 5.4 %bitcast_convert_fusion = f32[512,3072]{1,0:T(8,128)} fusion(bf16[8,4,16,3072]{3,2,1,0:T(8,128)(2,1)} %copy-done.2), kind=kLoop, calls=%fused_computation.70 | loop fusion | flops 1572864 | bytes 9437184 | tf_op jit(solution)/shard_map/convert_element_type | solution.py:88
  281.3 90.1 %reduce-scatter.2.cloned.1.call-done = f32[512,384]{1,0:T(8,128)} async-done(((f32[512,3072]{1,0:T(8,128)}), f32[512,384]{1,0:T(8,128)}) %reduce-scatter.2.cloned.1.call-update) | async-done | bytes 786448 | tf_op jit(solution)/shard_map/reduce_scatter | solution.py:124
  371.4 2.3 multiply_convert_fusion
  (61 shorter events, 4.8 us)
Async XLA Ops:
  6.5 85.4 %copy-start = (bf16[512,3072]{1,0:T(8,128)(2,1)S(1)}, bf16[512,3072]{1,0:T(8,128)(2,1)}, u32[]{:S(2)}) copy-start(bf16[512,3072]{1,0:T(8,128)(2,1)} %param.21) | copy-start | bytes 9437188
  10.1 9.5 %collective-permute-start = (f32[2,16,512]{2,1,0:T(8,128)S(1)}, f32[2,16,512]{2,1,0:T(8,128)S(1)}, u32[]{:S(2)}, u32[]{:S(2)}) collective-permute-start(f32[2,16,512]{2,1,0:T(8,128)S(1)} %constant_dynamic-slice_fusion), channel_id=1, source_target_pairs={{0,16},{16,32},{32,48},{48,64},{64,80},{80,96},{96,112},{1,17},{17... | collective-permute-start | bytes 196616 | tf_op jit(solution)/shard_map/ppermute | solution.py:14
  95.5 42.1 %all-to-all-start = ((bf16[8,4,16,3072]{3,2,1,0:T(8,128)(2,1)}), bf16[8,4,16,3072]{3,2,1,0:T(8,128)(2,1)S(1)}, u32[]{:S(2)}, u32[]{:S(2)}) async-start(bf16[8,4,16,3072]{3,2,1,0:T(8,128)(2,1)} %stack.2), calls=%async_computation | async-start | bytes 6291456 | tf_op jit(solution)/shard_map/all_to_all | solution.py:81
  99.9 10.5 %copy-start.8 = (f32[3072]{0:T(1024)S(1)}, f32[3072]{0:T(1024)}, u32[]{:S(2)}) copy-start(f32[3072]{0:T(1024)} %param.24) | copy-start | bytes 36868
  99.9 103.5 %all-gather.5.cloned.1.call-start = ((), (), s32[]{:S(2)}) async-start(), calls=%async_computation.3 | async-start | bytes 6684672 | tf_op jit(solution)/shard_map/all_gather | solution.py:103
  110.5 28.7 %copy-start.7 = (f32[3072]{0:T(1024)S(1)}, f32[3072]{0:T(1024)}, u32[]{:S(2)}) copy-start(f32[3072]{0:T(1024)} %param.23) | copy-start | bytes 36868
  137.6 3.2 copy-start.2
  137.6 4.1 %copy-start.3 = (bf16[3072,3,384]{0,2,1:T(8,128)(2,1)S(1)}, bf16[3072,3,384]{0,2,1:T(8,128)(2,1)}, u32[]{:S(2)}) copy-start(bf16[3072,3,384]{0,2,1:T(8,128)(2,1)} %copy.19) | copy-start | bytes 21233668
  146.0 1.4 copy-start.5
  146.0 2.1 copy-start.9
  149.1 99.2 %all-gather.3.cloned.1.call-start = ((), (), s32[]{:S(2)}) async-start(), calls=%async_computation.2 | async-start | bytes 6684672 | tf_op jit(solution)/shard_map/all_gather | solution.py:104
  151.3 220.1 %reduce-scatter.2.cloned.1.call-start = ((), (), s32[]{:S(2)}) async-start(), calls=%async_computation.4 | async-start | bytes 7077888 | tf_op jit(solution)/shard_map/reduce_scatter | solution.py:124
  151.8 51.7 %copy-start.6 = (f32[128]{0:T(128)S(1)}, f32[128]{0:T(128)}, u32[]{:S(2)}) copy-start(f32[128]{0:T(128)} %param.27) | copy-start | bytes 1540
  248.4 22.0 %copy-start.4 = (bf16[384,3072]{1,0:T(8,128)(2,1)S(1)}, bf16[384,3072]{1,0:T(8,128)(2,1)}, u32[]{:S(2)}) copy-start(bf16[384,3072]{1,0:T(8,128)(2,1)} %param.29) | copy-start | bytes 7077892
  275.0 98.7 %copy-start.1 = (bf16[512,3072]{1,0:T(8,128)(2,1)S(1)}, bf16[512,3072]{1,0:T(8,128)(2,1)}, u32[]{:S(2)}) copy-start(bf16[512,3072]{1,0:T(8,128)(2,1)} %param.21) | copy-start | bytes 9437188
Sparse Core Ops, SparseCore 0:
  149.3 40.1 all-gather.4
  191.1 43.1 all-gather.2
  275.1 96.2 reduce-scatter.1
